TPU v7x, 128 devices: a whole 4x4x4 slice. The times are simulated.
128 devices in a mesh: ctx: 16 (over x_lo, z, core), mp: 4 (over y), rep: 2 (over x_hi).
Axes of the slice: x: 4 (x_hi: 2, x_lo: 2; x = x_hi * 2 + x_lo), y: 4, z: 4, core: 2. Of those that a mesh axis runs over, the one named last changes fastest.
Arguments:
- token_pages: bfloat16 [128, 128, 2048], P('ctx'), may hold values from -13 to 13
- page_table: int32 [128], P('ctx'), may hold values from 0 to 7, as said below
- live_flags: int32 [128], P('ctx'), may hold values from 0 to 1, as said below
- lengths: int32 [32], replicated, may hold values from 1 to 1024, as said below
- decay_floor: float32 [2048], P(('mp', 'rep')), may hold values from 0.85 to 0.9998
- mixer_gain: float32 [2048], replicated, may hold values from 0.5 to 1.5
- feed_gain: float32 [2048], replicated, may hold values from 0.5 to 1.5
- trainer_mixer_in: float32 [3, 2048, 2048], P(None, ('ctx', 'mp')), may hold values from -0.125 to 0.125
- trainer_mixer_out: float32 [2048, 2048], P(None, ('ctx', 'mp')), may hold values from -0.125 to 0.125
- trainer_gate_up: float32 [2, 2048, 5632], P(None, ('ctx', 'mp')), may hold values from -0.125 to 0.125
- trainer_down: float32 [5632, 2048], P(None, ('ctx', 'mp')), may hold values from -0.078125 to 0.078125
Outputs:
- layer_output: bfloat16 [16384, 2048], P(('ctx', 'rep'), 'mp')
Inputs may be any that keep to these rules, and one draw needn't show every extreme that they name: `page_table`: within each device's block of 8 entries every value 0 to 7 appears once. `live_flags`: in each device's block of 8 flags at least half (rounded down, and never fewer than one) are ones, and some device's block is all ones. The lengths sum to 128 times the number of ones in live_flags; one prompt has exactly 1024 tokens.
All inputs are finite; a program needn't handle non-finite values.
Results may differ from a plain program's by a relative error of at most 0.015.
Values may be sent and summed in bfloat16 or wider, within the bound.
A program may use at most 192 MiB of HBM per device.

v0:
```python
import jax
import jax.numpy as jnp
from jax import lax
from jax.sharding import PartitionSpec as P

D = 2048
HEADS = 16
norm_eps = 1e-05


def prefix(value, axis, join, neutral):
    count, mine = (lax.axis_size(axis), lax.axis_index(axis))
    pieces = lax.all_gather(value, axis)
    total = jnp.full_like(value, 0) + jnp.asarray(neutral, value.dtype)

    def prefix_step(position, total):
        longer = join(total, pieces[position])
        return jnp.where(position < mine, longer, total)

    return lax.fori_loop(0, count - 1, prefix_step, total)


def entering_2(shard, axis, combine, identity):
    peers, position = (lax.axis_size(axis), lax.axis_index(axis))
    everything = jax.tree.map(
        lambda part, kind: lax.all_gather(part.astype(kind), axis),
        shard,
        (jnp.bfloat16, jnp.bfloat16),
    )
    start = jax.tree.map(
        lambda part, zero: jnp.broadcast_to(jnp.asarray(zero, part.dtype), part.shape),
        shard,
        identity,
    )

    def entering_step(k, before):
        reached = k < position
        new = combine(
            before, jax.tree.map(lambda part, own: part[k].astype(own.dtype), everything, shard)
        )
        return jax.tree.map(lambda a, b: jnp.where(reached, a, b), new, before)

    return lax.fori_loop(0, peers, entering_step, start)


def rms_scale(values_in, gain):
    mean_sq = jnp.mean(values_in * values_in, axis=-1, keepdims=True)
    return values_in * lax.rsqrt(mean_sq + norm_eps) * gain


def block_recurrence(queries, keys_in, values_in, log_decay, reset_count, state_init, count_init):
    highest = lax.Precision.HIGHEST

    def advance(carried_in, block_data):
        state, count_before = carried_in
        q_block, k_block, v_block, decay_block, count_block = block_data
        cumulative = jnp.cumsum(decay_block, axis=0)
        q_scaled = q_block * jnp.exp(cumulative)
        k_scaled = k_block * jnp.exp(-cumulative)
        scores = jnp.einsum("thd,shd->hts", q_scaled, k_scaled, precision=highest)
        positions = jnp.arange(count_block.shape[0])
        allowed = (positions[:, None] >= positions[None, :]) & (
            count_block[:, None] == count_block[None, :]
        )
        scores = jnp.where(allowed[None], scores, 0.0)
        outputs = jnp.einsum("hts,shd->thd", scores, v_block, precision=highest)
        from_state = jnp.einsum("thd,hde->the", q_scaled, state, precision=highest)
        outputs = outputs + jnp.where((count_block == count_before)[:, None, None], from_state, 0.0)
        last_count = count_block[-1]
        final_cum = cumulative[-1]
        weight_keys = (
            k_block
            * jnp.exp(final_cum[None] - cumulative)
            * (count_block == last_count).astype(k_block.dtype)[:, None, None]
        )
        retained = jnp.where(
            last_count == count_before, jnp.exp(final_cum)[:, :, None] * state, 0.0
        )
        state_next = retained + jnp.einsum("thd,the->hde", weight_keys, v_block, precision=highest)
        return ((state_next, last_count), outputs)

    final_carry, outputs_all = lax.scan(
        advance, (state_init, count_init), (queries, keys_in, values_in, log_decay, reset_count)
    )
    return (outputs_all, final_carry[0])


def compose_states(earlier, later):
    return (earlier[0] * later[0], later[0][:, :, None] * earlier[1] + later[1])


def add_counts(earlier, later):
    return earlier + later


def shards(
    token_pages,
    page_table,
    live_flags,
    lengths,
    decay_floor,
    mixer_gain,
    feed_gain,
    trainer_mixer_in,
    trainer_mixer_out,
    trainer_gate_up,
    trainer_down,
):
    mp_count = lax.axis_size("mp")
    rep_count = lax.axis_size("rep")
    mp_index = lax.axis_index("mp")
    rep_index = lax.axis_index("rep")
    width_local = trainer_mixer_in.shape[1]
    model_width = trainer_mixer_in.shape[2]
    head_cols = decay_floor.shape[0]
    head_dim = D // HEADS
    local_heads = head_cols // head_dim
    hidden_block = trainer_gate_up.shape[2] // mp_count
    mixer_in = lax.dynamic_index_in_dim(
        trainer_mixer_in.reshape(3, width_local, mp_count, rep_count, head_cols),
        rep_index,
        3,
        keepdims=False,
    )
    mixer_in = jnp.transpose(mixer_in, (1, 2, 0, 3)).reshape(width_local, mp_count, 3 * head_cols)
    mixer_out = lax.dynamic_index_in_dim(
        trainer_mixer_out.reshape(mp_count, rep_count, head_cols, width_local),
        rep_index,
        1,
        keepdims=False,
    )
    mixer_out = jnp.transpose(mixer_out, (2, 0, 1))
    gate_up = trainer_gate_up.reshape(2, width_local, mp_count, hidden_block)
    down_rows = trainer_down.reshape(mp_count, hidden_block, width_local)
    gate_up = jnp.transpose(gate_up, (1, 2, 0, 3)).reshape(width_local, mp_count, 2 * hidden_block)
    down_rows = jnp.transpose(down_rows, (2, 0, 1))
    packed = jnp.concatenate([mixer_in, mixer_out, gate_up, down_rows], axis=2).astype(jnp.bfloat16)
    arrived = lax.all_to_all(packed, "mp", split_axis=1, concat_axis=0, tiled=True)
    arrived = arrived.reshape(mp_count * width_local, packed.shape[2])
    served = lax.all_gather(arrived, "ctx", axis=0, tiled=True)
    w_mixer = served[:, : 3 * head_cols]
    w_output_t = served[:, 3 * head_cols : 4 * head_cols]
    feed_weights = served[:, 4 * head_cols :].reshape(model_width, 3, hidden_block)
    pages_local = token_pages.shape[0]
    page_len = token_pages.shape[1]
    tok_count = pages_local * page_len
    ordered = jnp.take(token_pages, page_table, axis=0).reshape(tok_count, model_width)
    live_tokens = jnp.repeat(live_flags, page_len)
    page_live = live_flags * page_len
    live_total = jnp.sum(page_live)
    stream_base = prefix(live_total, "ctx", add_counts, jnp.zeros((), jnp.int32))
    page_start = stream_base + jnp.cumsum(page_live) - page_live
    positions = (page_start[:, None] + jnp.arange(page_len, dtype=jnp.int32)[None, :]).reshape(
        tok_count
    )
    starts = jnp.cumsum(lengths) - lengths
    resets = (live_tokens == 1) & jnp.any(positions[:, None] == starts[None, :], axis=1)
    reset_count = jnp.cumsum(resets.astype(jnp.int32))
    live_float = live_tokens.astype(jnp.float32)[:, None]
    normed = rms_scale(ordered.astype(jnp.float32), mixer_gain).astype(jnp.bfloat16)
    projected = jnp.dot(normed, w_mixer, preferred_element_type=jnp.float32).reshape(
        tok_count, 3, head_cols
    )
    queries = jax.nn.silu(projected[:, 0])
    forget = decay_floor + (1.0 - decay_floor) * jax.nn.sigmoid(projected[:, 1])
    log_decay = jnp.log(forget) * live_float
    keys_in = (1.0 - forget) * live_float
    values_in = projected[:, 2]
    shape_blocks = (pages_local, page_len, local_heads, head_dim)
    local_out, local_state = block_recurrence(
        queries.reshape(shape_blocks),
        keys_in.reshape(shape_blocks),
        values_in.reshape(shape_blocks),
        log_decay.reshape(shape_blocks),
        reset_count.reshape(pages_local, page_len),
        jnp.zeros((local_heads, head_dim, head_dim), jnp.float32),
        jnp.zeros((), jnp.int32),
    )
    device_decay = jnp.where(
        reset_count[-1] == 0, jnp.exp(jnp.sum(log_decay, axis=0)), 0.0
    ).reshape(local_heads, head_dim)
    identity = (
        jnp.ones((local_heads, head_dim), jnp.float32),
        jnp.zeros((local_heads, head_dim, head_dim), jnp.float32),
    )
    entering = entering_2((device_decay, local_state), "ctx", compose_states, identity)[1]
    cum_device = jnp.cumsum(log_decay, axis=0).reshape(tok_count, local_heads, head_dim)
    scaled_queries = queries.reshape(tok_count, local_heads, head_dim) * jnp.exp(cum_device)
    correction = jnp.einsum(
        "thd,hde->the", scaled_queries, entering, precision=lax.Precision.HIGHEST
    )
    mixed = local_out.reshape(tok_count, local_heads, head_dim) + jnp.where(
        (reset_count == 0)[:, None, None], correction, 0.0
    )
    head_normed = (
        (mixed * lax.rsqrt(jnp.mean(mixed * mixed, axis=-1, keepdims=True) + norm_eps))
        .reshape(tok_count, head_cols)
        .astype(jnp.bfloat16)
    )
    half_rows = tok_count // rep_count
    col_block = model_width // mp_count
    attn_term = lax.dot_general(
        head_normed, w_output_t, (((1,), (1,)), ((), ())), preferred_element_type=jnp.float32
    )
    attn_all = lax.psum(attn_term.astype(jnp.bfloat16), ("mp", "rep")).astype(jnp.float32)
    residual = lax.dynamic_slice_in_dim(ordered, rep_index * half_rows, half_rows, 0).astype(
        jnp.float32
    ) + lax.dynamic_slice_in_dim(attn_all, rep_index * half_rows, half_rows, 0)
    feed_in = rms_scale(residual, feed_gain).astype(jnp.bfloat16)
    gated = jnp.einsum(
        "td,dcf->tcf", feed_in, feed_weights[:, :2], preferred_element_type=jnp.float32
    )
    hidden = (jax.nn.silu(gated[:, 0]) * gated[:, 1]).astype(jnp.bfloat16)
    down_term = lax.dot_general(
        hidden, feed_weights[:, 2], (((1,), (1,)), ((), ())), preferred_element_type=jnp.float32
    )
    summed = lax.psum_scatter(
        down_term.astype(jnp.bfloat16), "mp", scatter_dimension=1, tiled=True
    ).astype(jnp.float32)
    summed = summed + lax.dynamic_slice_in_dim(residual, mp_index * col_block, col_block, 1)
    live_half = lax.dynamic_slice_in_dim(live_tokens, rep_index * half_rows, half_rows, 0)
    return jnp.where(live_half[:, None] == 1, summed, 0.0).astype(jnp.bfloat16)


def solution(mesh):
    in_specs = (
        P("ctx", None, None),
        P("ctx"),
        P("ctx"),
        P(),
        P(("mp", "rep")),
        P(),
        P(),
        P(None, ("ctx", "mp"), None),
        P(None, ("ctx", "mp")),
        P(None, ("ctx", "mp"), None),
        P(None, ("ctx", "mp")),
    )
    out_specs = P(("ctx", "rep"), "mp")
    return jax.shard_map(shards, mesh=mesh, in_specs=in_specs, out_specs=out_specs, check_vma=False)
```

profile of v0, /device:TPU:1, one launch (start us, length us, event | category | flops | bytes accessed | tf_op | source)
XLA Modules:
  0.0 575.1 jit_solution(12584117254873081062)
XLA Ops:
  6.5 1.4 reshape.427
  8.4 1.0 reshape.429
  11.2 1.2 convert.27
  12.5 22.0 %all_to_all.15 = bf16[32,4,5248]{2,0,1:T(8,128)(2,1)} all-to-all(bf16[32,4,5248]{2,0,1:T(8,128)(2,1)S(1)} %pad_maximum_fusion), channel_id=1, replica_groups=mesh['ctx'=16,'mp'=4,'rep'=2] {'mp'}, dimensions={1} | all-to-all | bytes 2686976 | tf_op jit(solution)/shard_map/all_to_all | solution.py:138
  36.3 1.3 dynamic-update-slice
  37.6 13.0 %all-reduce = s32[16]{0:T(128)S(1)} all-reduce(s32[16]{0:T(128)S(1)} %dynamic-update-slice), channel_id=1, replica_groups=mesh['ctx'=16,'mp'=4,'rep'=2] {'ctx'}, use_global_device_ids=true, to_apply=%add | all-reduce | flops 16 | bytes 128
  50.7 18.5 %while.42 = (s32[]{:T(128)}, s32[]{:T(128)}, s32[]{:T(128)}, s32[16]{0:T(128)S(1)}, s32[]{:T(128)}) while((s32[]{:T(128)}, s32[]{:T(128)}, s32[]{:T(128)}, s32[16]{0:T(128)S(1)}, s32[]{:T(128)}) %tuple.96), condition=%wide.region_3.4_spmd, body=%wide.region_2.3_spmd.sunk | while | flops 5 | bytes 107 | solution.py:20
  69.8 5.1 gather_fusion
  75.1 3.6 fusion.21
  78.7 3.3 fusion.23
  82.0 68.7 %all-gather.4.cloned.1.call-done = bf16[2048,5248]{1,0:T(8,128)(2,1)} async-done(((bf16[128,5248]{1,0:T(8,128)(2,1)}), bf16[2048,5248]{1,0:T(8,128)(2,1)}) %all-gather.4.cloned.1.call-update) | async-done | bytes 21495824 | tf_op jit(solution)/shard_map/all_gather | solution.py:140
  150.8 2.1 slice_bitcast_fusion.3
  152.9 3.0 copy.104
  155.8 6.2 %fusion.62 = f32[1024,3,256]{2,0,1:T(8,128)S(1)} fusion(bf16[1024,2048,1]{1,0,2:T(8,128)(2,1)} %bitcast.193, bf16[3,256,2048]{2,1,0:T(8,128)(2,1)} %bitcast.197), kind=kOutput, calls=%fused_computation.127 | convolution fusion | flops 3221225472 | bytes 10485760 | tf_op jit(solution)/shard_map/dot_general | solution.py:161
  162.1 1.7 copy-done.2
  163.7 1.7 fusion.60
  165.4 1.7 div.45
  167.1 1.5 squeeze.62
  168.6 3.3 divide_multiply_fusion
  171.9 2.8 reshape_squeeze.3
  174.7 2.4 subtract_multiply_fusion
  177.1 95.7 %while.43 = (s32[]{:T(128)}, f32[2,128,128]{2,1,0:T(8,128)S(1)}, s32[]{:T(128)}, f32[8,128,2,128]{1,0,3,2:T(8,128)}, s32[8,128]{1,0:T(8,128)S(1)}, /*index=5*/f3...) while((s32[]{:T(128)}, f32[2,128,128]{2,1,0:T(8,128)S(1)}, ...), condition=%wide.region_11.12_spmd.clone, body=%wide.region_9.11_spmd.clone.sunk | while | flops 205996416 | bytes 3712938 | solution.py:82
  178.4 1.0 fusion.88
  179.4 1.2 bitcast_multiply_fusion.5
  182.7 4.8 dynamic_update_slice.6
  190.3 1.0 fusion.88
  191.4 1.2 bitcast_multiply_fusion.5
  194.7 4.8 dynamic_update_slice.6
  202.3 1.0 fusion.88
  203.4 1.2 bitcast_multiply_fusion.5
  206.6 4.8 dynamic_update_slice.6
  214.3 1.0 fusion.88
  215.3 1.2 bitcast_multiply_fusion.5
  218.6 4.8 dynamic_update_slice.6
  226.3 1.0 fusion.88
  227.3 1.2 bitcast_multiply_fusion.5
  230.6 4.8 dynamic_update_slice.6
  238.2 1.0 fusion.88
  239.3 1.2 bitcast_multiply_fusion.5
  242.5 4.8 dynamic_update_slice.6
  250.2 1.0 fusion.88
  251.2 1.2 bitcast_multiply_fusion.5
  254.5 4.8 dynamic_update_slice.6
  262.2 1.0 fusion.88
  263.2 1.2 bitcast_multiply_fusion.5
  266.5 4.8 dynamic_update_slice.6
  275.5 2.4 reshape.434
  277.9 1.7 fusion.58
  280.8 1.4 copy.111
  282.2 18.9 %all_gather.22 = bf16[16,2,128]{2,1,0:T(2,128)(2,1)S(1)} all-gather(bf16[1,2,128]{2,1,0:T(2,128)(2,1)S(1)} %fusion.52), channel_id=1, replica_groups=mesh['ctx'=16,'mp'=4,'rep'=2] {'ctx'}, dimensions={0}, use_global_device_ids=true | all-gather | bytes 8704 | tf_op jit(solution)/shard_map/all_gather | solution.py:26
  301.1 6.1 %all-gather.6.cloned.1.call-done = bf16[32,128,128]{2,1,0:T(8,128)(2,1)} async-done(((bf16[2,128,128]{2,1,0:T(8,128)(2,1)}), bf16[32,128,128]{2,1,0:T(8,128)(2,1)}) %all-gather.6.cloned.1.call-update) | async-done | bytes 1048592 | tf_op jit(solution)/shard_map/all_gather | solution.py:26
  307.2 16.2 %while.44 = (s32[]{:T(128)}, f32[2,128,128]{2,1,0:T(8,128)S(1)}, s32[]{:T(128)}, bf16[16,2,128]{2,1,0:T(2,128)(2,1)S(1)}, bf16[16,2,128,128]{3,2,1,0:T(8,128)(2,1)}, /*index=5*/s32[]{:T(128)}, s32[]{:T(128)}) while((s32[]{:T(128)}, f32[2,128,128]{2,1,0:T(8,128)S(1)}, s32[]{:T(128)}, bf16[16,2,128]{2,1,0:T(2,128)(2,1)S(1)}, ...), condition=%wide.region_14.15_spmd.clone, body=%wide.region_13.14_spmd.clone.sunk | while | flops 164100 | bytes 330345 | solution.py:43
  308.2 1.0 fusion.93
  309.2 1.0 fusion.93
  323.4 2.9 multiply_reduce_fusion.1
  326.4 4.5 convolution_convert_fusion
  331.2 14.2 %slice.81 = bf16[2048,4224]{1,0:T(8,128)(2,1)} slice(bf16[2048,5248]{1,0:T(8,128)(2,1)} %all-gather.4.cloned.1.call-done), slice={[0:2048], [1024:5248]} | slice | bytes 34603008 | tf_op jit(solution)/shard_map/slice | solution.py:143
  345.4 22.6 %copy.114 = bf16[2048,4224]{0,1:T(8,128)(2,1)} copy(bf16[2048,4224]{1,0:T(8,128)(2,1)} %slice.81) | data formatting | bytes 34603008 | tf_op jit(solution)/shard_map/slice | solution.py:143
  368.0 147.3 %all-reduce.3.cloned.1.call-done = bf16[1024,2048]{1,0:T(8,128)(2,1)} async-done(((bf16[1024,2048]{1,0:T(8,128)(2,1)}), bf16[1024,2048]{1,0:T(8,128)(2,1)}) %all-reduce.3.cloned.1.call-update) | async-done | bytes 4194320 | tf_op jit(solution)/shard_map/psum | solution.py:205
  515.3 3.2 multiply_reduce_fusion
  518.5 11.2 %fusion.19 = f32[512,2,1408]{2,0,1:T(8,128)S(1)} fusion(bf16[2048,3,1408]{0,2,1:T(8,128)(2,1)} %bitcast.190, f32[512,2048]{1,0:T(8,128)S(1)} %get-tuple-element.362, f32[2048]{0:T(1024)S(1)} %copy-done.9, f32[512]{0:T(512)S(1)} %add_rsqrt_fusion.2), kind=kOutput, calls=%fused_computation.36 | convolution fusion | flops 5908725760 | bytes 21506048 | tf_op jit(solution)/shard_map/td,dcf->tcf/dot_general | solution.py:210
  529.7 7.3 %fusion.25 = bf16[512,2048]{1,0:T(8,128)(2,1)} fusion(bf16[2048,3,1408]{0,2,1:T(8,128)(2,1)} %bitcast.191, f32[512,2,1408]{2,0,1:T(8,128)S(1)} %fusion.19), kind=kOutput, calls=%fused_computation.51 | convolution fusion | flops 2958163968 | bytes 13631488 | tf_op jit(solution)/shard_map/dot_general | solution.py:214
  537.2 29.1 %reduce-scatter.2.cloned.1.call-done = bf16[512,512]{1,0:T(8,128)(2,1)} async-done(((bf16[512,2048]{1,0:T(8,128)(2,1)}), bf16[512,512]{1,0:T(8,128)(2,1)}) %reduce-scatter.2.cloned.1.call-update) | async-done | bytes 524304 | tf_op jit(solution)/shard_map/reduce_scatter | solution.py:217
  566.3 2.3 select_convert_fusion
  (223 shorter events, 60.3 us)
Async XLA Ops:
  6.5 3.1 copy-start.3
  6.5 144.2 %all-gather.4.cloned.1.call-start = ((), (), s32[]{:S(2)}) async-start(), calls=%async_computation.2 | async-start | bytes 22839296 | tf_op jit(solution)/shard_map/all_gather | solution.py:140
  11.1 23.5 %copy-start.6 = (s32[8]{0:T(128)S(1)}, s32[8]{0:T(128)}, u32[]{:S(2)}) copy-start(s32[8]{0:T(128)} %param.19) | copy-start | bytes 100
  11.1 23.5 %copy-start.8 = (s32[8]{0:T(128)S(1)}, s32[8]{0:T(128)}, u32[]{:S(2)}) copy-start(s32[8]{0:T(128)} %param.18) | copy-start | bytes 100
  11.2 24.3 %copy-start.7 = (s32[32]{0:T(128)S(1)}, s32[32]{0:T(128)}, u32[]{:S(2)}) copy-start(s32[32]{0:T(128)} %param.20) | copy-start | bytes 388
  11.2 24.6 %copy-start.10 = (u32[128]{0:T(128)S(1)}, u32[128]{0:T(128)}, u32[]{:S(2)}) copy-start(u32[128]{0:T(128)} %constant.161) | copy-start | bytes 1540
  34.5 272.6 %all-gather.6.cloned.1.call-start = ((), (), s32[]{:S(2)}) async-start(), calls=%async_computation.5 | async-start | bytes 1114112 | tf_op jit(solution)/shard_map/all_gather | solution.py:26
  69.8 5.2 copy-start.4
  74.9 3.8 copy-start
  74.9 3.8 copy-start.5
  162.1 1.7 copy-start.2
  273.5 241.7 %all-reduce.3.cloned.1.call-start = ((), (), s32[]{:S(2)}) async-start(), calls=%async_computation.3 | async-start | bytes 8388608 | tf_op jit(solution)/shard_map/psum | solution.py:205
  331.0 235.3 %reduce-scatter.2.cloned.1.call-start = ((), (), s32[]{:S(2)}) async-start(), calls=%async_computation.4 | async-start | bytes 2621440 | tf_op jit(solution)/shard_map/reduce_scatter | solution.py:217
  515.3 3.2 copy-start.9
  518.5 11.2 %copy-start.1 = (f32[512,2048]{1,0:T(8,128)}, f32[512,2048]{1,0:T(8,128)S(1)}, u32[]{:S(2)}) copy-start(f32[512,2048]{1,0:T(8,128)S(1)} %get-tuple-element.362) | copy-start | bytes 12582916
Sparse Core Ops, SparseCore 0:
  34.7 116.0 all-gather.3
  273.7 33.4 all-gather.5
  331.1 184.1 all-reduce.2
  537.2 29.0 reduce-scatter.1
where the time goes:
time: 578 us; the launch traced here: 575 us
  waiting for transfers between devices  251 us (43%)
  local copies, waits for them, and re-layouts  127 us (22%)
  other arithmetic  65.4 us (11%)
  blocking collectives  54 us (9%)
  matrix products  42.7 us (7%)
  loops' own time  20.7 us (4%)
  between operations  14.2 us (2%)
    psum x1, waiting for transfers between devices, shards(): lax.psum(attn_term.astype(jnp.bfloat16), ('mp', 'rep')).astype(jnp.float32)  147 us
    all_gather x1, waiting for transfers between devices, shards(): served = lax.all_gather(arrived, 'ctx', axis=0, tiled=True)  68.7 us
    dynamic_update_slice x16, local copies, waits for them, and re-layouts, block_recurrence(): lax.scan(advance, (state_init, count_init), (queries, keys_in, values_in,...  38.8 us
    slice x2, local copies, waits for them, and re-layouts, shards(): served[:, 4 * head_cols:].reshape(model_width, 3, hidden_block)  36.8 us
    reduce_scatter x1, waiting for transfers between devices, shards(): lax.psum_scatter(down_term.astype(jnp.bfloat16), 'mp', scatter_dimension=...  29.1 us
    all_to_all x1, blocking collectives, shards(): lax.all_to_all(packed, 'mp', split_axis=1, concat_axis=0, tiled=True)  22 us
    all_gather x1, blocking collectives, entering_2(): lax.all_gather(part.astype(kind), axis)  18.9 us
    select_n x16, other arithmetic, entering_step(): return jax.tree.map(lambda a, b: jnp.where(reached, a, b), new, before)  15.5 us
  transfers between devices with their start and end apart: 4, of which 4 were waited for; matrix products, arithmetic and copies ran while one was open for 12% of the time, Pallas kernels for 0%

commit v1 on v0

--- a/solution.py
+++ b/solution.py
@@ -135,7 +135,16 @@
     gate_up = jnp.transpose(gate_up, (1, 2, 0, 3)).reshape(width_local, mp_count, 2 * hidden_block)
     down_rows = jnp.transpose(down_rows, (2, 0, 1))
     packed = jnp.concatenate([mixer_in, mixer_out, gate_up, down_rows], axis=2).astype(jnp.bfloat16)
-    arrived = lax.all_to_all(packed, "mp", split_axis=1, concat_axis=0, tiled=True)
+
+    def _define_group(base_x):
+        return jnp.concatenate(
+            lax.all_to_all(
+                jnp.stack(jnp.split(base_x, lax.axis_size("mp"), axis=1), axis=0), "mp", 0, 0
+            ),
+            axis=0,
+        )
+
+    arrived = _define_group(packed)
     arrived = arrived.reshape(mp_count * width_local, packed.shape[2])
     served = lax.all_gather(arrived, "ctx", axis=0, tiled=True)
     w_mixer = served[:, : 3 * head_cols]

time: 578 us -> 579 us (level)
  no operation moved by 1% of the time
where the time goes in v1:
time: 579 us; the launch traced here: 575 us
  waiting for transfers between devices  253 us (44%)
  local copies, waits for them, and re-layouts  125 us (22%)
  other arithmetic  65.6 us (11%)
  blocking collectives  54 us (9%)
  matrix products  42.7 us (7%)
  loops' own time  20.7 us (4%)
  between operations  14.2 us (2%)
    psum x1, waiting for transfers between devices, shards(): lax.psum(attn_term.astype(jnp.bfloat16), ('mp', 'rep')).astype(jnp.float32)  147 us
    all_gather x1, waiting for transfers between devices, shards(): served = lax.all_gather(arrived, 'ctx', axis=0, tiled=True)  68.7 us
    dynamic_update_slice x16, local copies, waits for them, and re-layouts, block_recurrence(): lax.scan(advance, (state_init, count_init), (queries, keys_in, values_in,...  38.8 us
    slice x2, local copies, waits for them, and re-layouts, shards(): served[:, 4 * head_cols:].reshape(model_width, 3, hidden_block)  36.8 us
    reduce_scatter x1, waiting for transfers between devices, shards(): lax.psum_scatter(down_term.astype(jnp.bfloat16), 'mp', scatter_dimension=...  29.1 us
    all_to_all x1, blocking collectives, _define_group(): lax.all_to_all(jnp.stack(jnp.split(base_x, lax.axis_size('mp'), axis=1),...  22 us
    all_gather x1, blocking collectives, entering_2(): lax.all_gather(part.astype(kind), axis)  19 us
    select_n x16, other arithmetic, entering_step(): return jax.tree.map(lambda a, b: jnp.where(reached, a, b), new, before)  15.5 us
  transfers between devices with their start and end apart: 4, of which 4 were waited for; matrix products, arithmetic and copies ran while one was open for 12% of the time, Pallas kernels for 0%

profile of v1, /device:TPU:1, one launch (start us, length us, event | category | flops | bytes accessed | tf_op | source)
XLA Modules:
  0.0 575.5 jit_solution(7016973023435856332)
XLA Ops:
  6.5 1.4 reshape.423
  8.4 1.0 reshape.425
  11.1 1.1 convert.27
  12.8 22.0 %all_to_all.5 = bf16[4,32,1,5248]{3,1,2,0:T(8,128)(2,1)} all-to-all(bf16[4,32,1,5248]{3,1,2,0:T(8,128)(2,1)S(1)} %pad_maximum_fusion.1), channel_id=1, replica_groups=mesh['ctx'=16,'mp'=4,'rep'=2] {'mp'}, dimensions={0} | all-to-all | bytes 2686976 | tf_op jit(solution)/shard_map/all_to_all | solution.py:141
  36.6 1.3 dynamic-update-slice
  37.9 13.0 %all-reduce = s32[16]{0:T(128)S(1)} all-reduce(s32[16]{0:T(128)S(1)} %dynamic-update-slice), channel_id=1, replica_groups=mesh['ctx'=16,'mp'=4,'rep'=2] {'ctx'}, use_global_device_ids=true, to_apply=%add | all-reduce | flops 16 | bytes 128
  51.0 18.5 %while.42 = (s32[]{:T(128)}, s32[]{:T(128)}, s32[]{:T(128)}, s32[16]{0:T(128)S(1)}, s32[]{:T(128)}) while((s32[]{:T(128)}, s32[]{:T(128)}, s32[]{:T(128)}, s32[16]{0:T(128)S(1)}, s32[]{:T(128)}) %tuple.99), condition=%wide.region_3.4_spmd, body=%wide.region_2.3_spmd.sunk | while | flops 5 | bytes 107 | solution.py:20
  70.1 5.1 gather_fusion
  75.4 3.6 fusion.21
  79.0 3.3 fusion.23
  82.3 68.7 %all-gather.4.cloned.1.call-done = bf16[2048,5248]{1,0:T(8,128)(2,1)} async-done(((bf16[128,5248]{1,0:T(8,128)(2,1)}), bf16[2048,5248]{1,0:T(8,128)(2,1)}) %all-gather.4.cloned.1.call-update) | async-done | bytes 21495824 | tf_op jit(solution)/shard_map/all_gather | solution.py:149
  151.1 2.1 slice_bitcast_fusion.3
  153.2 3.0 copy.107
  156.1 6.2 %fusion.62 = f32[1024,3,256]{2,0,1:T(8,128)S(1)} fusion(bf16[1024,2048,1]{1,0,2:T(8,128)(2,1)} %bitcast.197, bf16[3,256,2048]{2,1,0:T(8,128)(2,1)} %bitcast.201), kind=kOutput, calls=%fused_computation.132 | convolution fusion | flops 3221225472 | bytes 10485760 | tf_op jit(solution)/shard_map/dot_general | solution.py:170
  162.4 1.7 copy-done.2
  164.0 1.7 fusion.60
  165.7 1.7 div.45
  167.4 1.5 squeeze.62
  168.9 3.3 divide_multiply_fusion
  172.2 2.8 reshape_squeeze.3
  175.0 2.4 subtract_multiply_fusion
  177.4 95.7 %while.43 = (s32[]{:T(128)}, f32[2,128,128]{2,1,0:T(8,128)S(1)}, s32[]{:T(128)}, f32[8,128,2,128]{1,0,3,2:T(8,128)}, s32[8,128]{1,0:T(8,128)S(1)}, /*index=5*/f3...) while((s32[]{:T(128)}, f32[2,128,128]{2,1,0:T(8,128)S(1)}, ...), condition=%wide.region_11.12_spmd.clone, body=%wide.region_9.11_spmd.clone.sunk | while | flops 205996416 | bytes 3712938 | solution.py:82
  178.7 1.0 fusion.88
  179.7 1.2 bitcast_multiply_fusion.5
  183.0 4.8 dynamic_update_slice.6
  190.6 1.0 fusion.88
  191.7 1.2 bitcast_multiply_fusion.5
  195.0 4.8 dynamic_update_slice.6
  202.6 1.0 fusion.88
  203.7 1.2 bitcast_multiply_fusion.5
  206.9 4.8 dynamic_update_slice.6
  214.6 1.0 fusion.88
  215.6 1.2 bitcast_multiply_fusion.5
  218.9 4.8 dynamic_update_slice.6
  226.5 1.0 fusion.88
  227.6 1.2 bitcast_multiply_fusion.5
  230.9 4.8 dynamic_update_slice.6
  238.5 1.0 fusion.88
  239.6 1.2 bitcast_multiply_fusion.5
  242.8 4.8 dynamic_update_slice.6
  250.5 1.0 fusion.88
  251.5 1.2 bitcast_multiply_fusion.5
  254.8 4.8 dynamic_update_slice.6
  262.5 1.0 fusion.88
  263.5 1.2 bitcast_multiply_fusion.5
  266.8 4.8 dynamic_update_slice.6
  275.4 1.4 copy.123
  276.8 1.7 fusion.58
  279.7 1.3 copy.114
  281.2 19.0 %all_gather.22 = bf16[16,2,128]{2,1,0:T(2,128)(2,1)S(1)} all-gather(bf16[1,2,128]{2,1,0:T(2,128)(2,1)S(1)} %fusion.52), channel_id=1, replica_groups=mesh['ctx'=16,'mp'=4,'rep'=2] {'ctx'}, dimensions={0}, use_global_device_ids=true | all-gather | bytes 8704 | tf_op jit(solution)/shard_map/all_gather | solution.py:26
  300.2 7.3 %all-gather.6.cloned.1.call-done = bf16[32,128,128]{2,1,0:T(8,128)(2,1)} async-done(((bf16[2,128,128]{2,1,0:T(8,128)(2,1)}), bf16[32,128,128]{2,1,0:T(8,128)(2,1)}) %all-gather.6.cloned.1.call-update) | async-done | bytes 1048592 | tf_op jit(solution)/shard_map/all_gather | solution.py:26
  307.5 16.2 %while.44 = (s32[]{:T(128)}, f32[2,128,128]{2,1,0:T(8,128)S(1)}, s32[]{:T(128)}, bf16[16,2,128]{2,1,0:T(2,128)(2,1)S(1)}, bf16[16,2,128,128]{3,2,1,0:T(8,128)(2,1)}, /*index=5*/s32[]{:T(128)}, s32[]{:T(128)}) while((s32[]{:T(128)}, f32[2,128,128]{2,1,0:T(8,128)S(1)}, s32[]{:T(128)}, bf16[16,2,128]{2,1,0:T(2,128)(2,1)S(1)}, ...), condition=%wide.region_14.15_spmd.clone, body=%wide.region_13.14_spmd.clone.sunk | while | flops 164100 | bytes 330345 | solution.py:43
  308.5 1.0 fusion.93
  309.5 1.0 fusion.93
  323.7 2.9 multiply_reduce_fusion.1
  326.8 4.5 convolution_convert_fusion
  331.5 14.2 %slice.81 = bf16[2048,4224]{1,0:T(8,128)(2,1)} slice(bf16[2048,5248]{1,0:T(8,128)(2,1)} %all-gather.4.cloned.1.call-done), slice={[0:2048], [1024:5248]} | slice | bytes 34603008 | tf_op jit(solution)/shard_map/slice | solution.py:152
  345.7 22.6 %copy.117 = bf16[2048,4224]{0,1:T(8,128)(2,1)} copy(bf16[2048,4224]{1,0:T(8,128)(2,1)} %slice.81) | data formatting | bytes 34603008 | tf_op jit(solution)/shard_map/slice | solution.py:152
  368.3 147.3 %all-reduce.3.cloned.1.call-done = bf16[1024,2048]{1,0:T(8,128)(2,1)} async-done(((bf16[1024,2048]{1,0:T(8,128)(2,1)}), bf16[1024,2048]{1,0:T(8,128)(2,1)}) %all-reduce.3.cloned.1.call-update) | async-done | bytes 4194320 | tf_op jit(solution)/shard_map/psum | solution.py:214
  515.6 3.2 multiply_reduce_fusion
  518.9 11.2 %fusion.19 = f32[512,2,1408]{2,0,1:T(8,128)S(1)} fusion(bf16[2048,3,1408]{0,2,1:T(8,128)(2,1)} %bitcast.194, f32[512,2048]{1,0:T(8,128)S(1)} %get-tuple-element.362, f32[2048]{0:T(1024)S(1)} %copy-done.10, f32[512]{0:T(512)S(1)} %add_rsqrt_fusion.2), kind=kOutput, calls=%fused_computation.36 | convolution fusion | flops 5908725760 | bytes 21506048 | tf_op jit(solution)/shard_map/td,dcf->tcf/dot_general | solution.py:219
  530.1 7.3 %fusion.25 = bf16[512,2048]{1,0:T(8,128)(2,1)} fusion(bf16[2048,3,1408]{0,2,1:T(8,128)(2,1)} %bitcast.195, f32[512,2,1408]{2,0,1:T(8,128)S(1)} %fusion.19), kind=kOutput, calls=%fused_computation.51 | convolution fusion | flops 2958163968 | bytes 13631488 | tf_op jit(solution)/shard_map/dot_general | solution.py:223
  537.5 29.1 %reduce-scatter.2.cloned.1.call-done = bf16[512,512]{1,0:T(8,128)(2,1)} async-done(((bf16[512,2048]{1,0:T(8,128)(2,1)}), bf16[512,512]{1,0:T(8,128)(2,1)}) %reduce-scatter.2.cloned.1.call-update) | async-done | bytes 524304 | tf_op jit(solution)/shard_map/reduce_scatter | solution.py:226
  566.6 2.3 select_convert_fusion
  (227 shorter events, 60.4 us)
Async XLA Ops:
  6.5 3.1 copy-start.3
  6.5 144.5 %all-gather.4.cloned.1.call-start = ((), (), s32[]{:S(2)}) async-start(), calls=%async_computation.2 | async-start | bytes 22839296 | tf_op jit(solution)/shard_map/all_gather | solution.py:149
  12.4 22.5 %copy-start.7 = (s32[8]{0:T(128)S(1)}, s32[8]{0:T(128)}, u32[]{:S(2)}) copy-start(s32[8]{0:T(128)} %param.19) | copy-start | bytes 100
  12.4 22.5 %copy-start.9 = (s32[8]{0:T(128)S(1)}, s32[8]{0:T(128)}, u32[]{:S(2)}) copy-start(s32[8]{0:T(128)} %param.18) | copy-start | bytes 100
  12.4 23.3 %copy-start.8 = (s32[32]{0:T(128)S(1)}, s32[32]{0:T(128)}, u32[]{:S(2)}) copy-start(s32[32]{0:T(128)} %param.20) | copy-start | bytes 388
  12.5 23.6 %copy-start.11 = (u32[128]{0:T(128)S(1)}, u32[128]{0:T(128)}, u32[]{:S(2)}) copy-start(u32[128]{0:T(128)} %constant.161) | copy-start | bytes 1540
  34.8 272.7 %all-gather.6.cloned.1.call-start = ((), (), s32[]{:S(2)}) async-start(), calls=%async_computation.5 | async-start | bytes 1114112 | tf_op jit(solution)/shard_map/all_gather | solution.py:26
  70.1 5.2 copy-start.5
  75.2 3.8 copy-start
  75.2 3.8 copy-start.6
  162.4 1.7 copy-start.2
  273.8 241.8 %all-reduce.3.cloned.1.call-start = ((), (), s32[]{:S(2)}) async-start(), calls=%async_computation.3 | async-start | bytes 8388608 | tf_op jit(solution)/shard_map/psum | solution.py:214
  278.4 2.6 copy-start.4
  331.3 235.3 %reduce-scatter.2.cloned.1.call-start = ((), (), s32[]{:S(2)}) async-start(), calls=%async_computation.4 | async-start | bytes 2621440 | tf_op jit(solution)/shard_map/reduce_scatter | solution.py:226
  515.6 3.2 copy-start.10
  518.9 11.2 %copy-start.1 = (f32[512,2048]{1,0:T(8,128)}, f32[512,2048]{1,0:T(8,128)S(1)}, u32[]{:S(2)}) copy-start(f32[512,2048]{1,0:T(8,128)S(1)} %get-tuple-element.362) | copy-start | bytes 12582916
Sparse Core Ops, SparseCore 0:
  35.0 116.0 all-gather.3
  274.0 33.5 all-gather.5
  331.4 184.1 all-reduce.2
  537.6 29.0 reduce-scatter.1
